TPU v7x, 32 devices: a whole 2x2x4 slice. The times are simulated.
32 devices in a mesh: dp: 16 (over z, y, x), fsdp: 2 (over core).
Axes of the slice: x: 2, y: 2, z: 4, core: 2. Of those that a mesh axis runs over, the one named last changes fastest.
Arguments:
- tokens: bfloat16 [32, 1024, 768], P(('dp', 'fsdp')), may hold values from -6 to 6
- cotangent: bfloat16 [32, 1024, 768], P(('dp', 'fsdp')), may hold values from -6 to 6
- segments: int32 [32, 1024], P(('dp', 'fsdp')), may hold values from 0 to 15, never falling along the last dimension, each value on 1 to 128 neighbouring positions
- keep_mask: int32 [32, 1024], P(('dp', 'fsdp')), may hold values 0 or 1
- qkv_weight: float32 [2, 768, 2304], P(None, 'fsdp'), may hold values from -0.21875 to 0.21875
- qkv_first: float32 [2, 768, 2304], P(None, 'fsdp'), may hold values from -512 to 512
- qkv_second: float32 [2, 768, 2304], P(None, 'fsdp'), may hold values from 4096 to 65536
- proj_weight: float32 [2, 768, 768], P(None, 'fsdp'), may hold values from -0.625 to 0.625
- proj_first: float32 [2, 768, 768], P(None, 'fsdp'), may hold values from -512 to 512
- proj_second: float32 [2, 768, 768], P(None, 'fsdp'), may hold values from 4096 to 65536
- up_weight: float32 [2, 768, 3072], P(None, 'fsdp'), may hold values from -0.21875 to 0.21875
- up_first: float32 [2, 768, 3072], P(None, 'fsdp'), may hold values from -512 to 512
- up_second: float32 [2, 768, 3072], P(None, 'fsdp'), may hold values from 4096 to 65536
- down_weight: float32 [2, 3072, 768], P(None, 'fsdp'), may hold values from -0.109375 to 0.109375
- down_first: float32 [2, 3072, 768], P(None, 'fsdp'), may hold values from -512 to 512
- down_second: float32 [2, 3072, 768], P(None, 'fsdp'), may hold values from 4096 to 65536
- norm_gains: float32 [2, 768, 4], P(None, 'fsdp'), may hold values from 0.5 to 1.5
- gains_first: float32 [2, 768, 4], P(None, 'fsdp'), may hold values from -512 to 512
- gains_second: float32 [2, 768, 4], P(None, 'fsdp'), may hold values from 4096 to 65536
Outputs:
- output: bfloat16 [32, 1024, 768], P(('dp', 'fsdp'))
- input_grad: float32 [32, 1024, 768], P(('dp', 'fsdp'))
- new_qkv_weight: float32 [2, 768, 2304], P(None, 'fsdp')
- new_qkv_first: float32 [2, 768, 2304], P(None, 'fsdp')
- new_qkv_second: float32 [2, 768, 2304], P(None, 'fsdp')
- new_proj_weight: float32 [2, 768, 768], P(None, 'fsdp')
- new_proj_first: float32 [2, 768, 768], P(None, 'fsdp')
- new_proj_second: float32 [2, 768, 768], P(None, 'fsdp')
- new_up_weight: float32 [2, 768, 3072], P(None, 'fsdp')
- new_up_first: float32 [2, 768, 3072], P(None, 'fsdp')
- new_up_second: float32 [2, 768, 3072], P(None, 'fsdp')
- new_down_weight: float32 [2, 3072, 768], P(None, 'fsdp')
- new_down_first: float32 [2, 3072, 768], P(None, 'fsdp')
- new_down_second: float32 [2, 3072, 768], P(None, 'fsdp')
- new_norm_gains: float32 [2, 768, 4], P(None, 'fsdp')
- new_gains_first: float32 [2, 768, 4], P(None, 'fsdp')
- new_gains_second: float32 [2, 768, 4], P(None, 'fsdp')
Inputs may be any that keep to these rules, and one draw needn't show every extreme that they name: `segments`: in each packed sequence the ids never fall, and each image holds 1 to 128 positions.
All inputs are finite; a program needn't handle non-finite values. No bound on the sum of `keep_mask` on one device may be relied on, other than what follows from the above.
Results may differ from a plain program's by a relative error of at most 0.035.
Values may be sent and summed in bfloat16 or wider, within the bound.
A program may use at most 512 MiB of HBM per device.

v0:
```python
import jax
import jax.numpy as jnp
from jax import lax
from jax.sharding import PartitionSpec as P

D = 768
HEADS = 12
HEAD_DIM = 64
STEP = 5
norm_eps = 1e-06
adam_eps = 1e-08


def layer_norm(values, gain):
    average = jnp.mean(values, axis=-1, keepdims=True)
    centred = values - average
    spread = jnp.mean(centred * centred, axis=-1, keepdims=True)
    return centred * lax.rsqrt(spread + norm_eps) * gain


def gelu_tanh(values):
    return jax.nn.gelu(values, approximate=True)


def allowed_pairs(seg_row, keep_row):
    positions = jnp.arange(seg_row.shape[0])
    diagonal = positions[:, None] == positions[None, :]
    return (seg_row[:, None] == seg_row[None, :]) & ((keep_row[None, :] == 1) | diagonal)


def key_window(start, span, length):
    reach = length // 8
    extent = min(length, span + 2 * reach)
    lower_key = max(0, min(start - reach, length - extent))
    return (lower_key, lower_key + extent)


def block_probs(query_block, keys_part, allowed_block, scale_factor):
    scores = (
        jnp.einsum("qhd,khd->hqk", query_block, keys_part, preferred_element_type=jnp.float32)
        * scale_factor
    )
    return jnp.where(allowed_block[None], scores, -1e30)


def attend_forward(queries, keys_all, values, allowed, span, scale_factor):
    length = queries.shape[0]
    outputs, peaks, totals = ([], [], [])
    for start in range(0, length, span):
        lower_key, upper_key = key_window(start, span, length)
        masked = block_probs(
            queries[start : start + span],
            keys_all[lower_key:upper_key],
            allowed[start : start + span, lower_key:upper_key],
            scale_factor,
        )
        peak = jnp.max(masked, axis=-1, keepdims=True)
        expo = jnp.exp(masked - peak)
        total = jnp.sum(expo, axis=-1, keepdims=True)
        probs = (expo / total).astype(jnp.bfloat16)
        outputs.append(
            jnp.einsum(
                "hqk,khd->qhd",
                probs,
                values[lower_key:upper_key],
                preferred_element_type=jnp.float32,
            ).astype(jnp.bfloat16)
        )
        peaks.append(peak)
        totals.append(total)
    return (jnp.concatenate(outputs, axis=0), peaks, totals)


def attend_backward(
    queries, keys_all, values, allowed, d_attended, peaks, totals, span, scale_factor
):
    length = queries.shape[0]
    d_keys = jnp.zeros(keys_all.shape, jnp.float32)
    d_values = jnp.zeros(values.shape, jnp.float32)
    d_query_parts = []
    for block_index, start in enumerate(range(0, length, span)):
        lower_key, upper_key = key_window(start, span, length)
        keys_part = keys_all[lower_key:upper_key]
        values_part = values[lower_key:upper_key]
        query_block = queries[start : start + span]
        d_block = d_attended[start : start + span]
        masked = block_probs(
            query_block, keys_part, allowed[start : start + span, lower_key:upper_key], scale_factor
        )
        probs_raw = jnp.exp(masked - peaks[block_index]) / totals[block_index]
        probs = probs_raw.astype(jnp.bfloat16)
        d_probs = jnp.einsum(
            "qhd,khd->hqk", d_block, values_part, preferred_element_type=jnp.float32
        )
        d_values = d_values.at[lower_key:upper_key].add(
            jnp.einsum("hqk,qhd->khd", probs, d_block, preferred_element_type=jnp.float32)
        )
        inner = jnp.sum(d_probs * probs_raw, axis=-1, keepdims=True)
        d_scores = (probs_raw * (d_probs - inner)).astype(jnp.bfloat16)
        d_query_parts.append(
            jnp.einsum("hqk,khd->qhd", d_scores, keys_part, preferred_element_type=jnp.float32)
            * scale_factor
        )
        d_keys = d_keys.at[lower_key:upper_key].add(
            jnp.einsum("hqk,qhd->khd", d_scores, query_block, preferred_element_type=jnp.float32)
            * scale_factor
        )
    return (jnp.concatenate(d_query_parts, axis=0), d_keys, d_values)


def layer_forward(hidden, gathered, allowed_rows, span, scale_factor):
    joint_mat, proj_mat, upper_mat, lower_mat, gain_set = gathered
    gains_wide = gain_set.astype(jnp.float32)
    normed = layer_norm(hidden, gains_wide[:, 0]).astype(jnp.bfloat16)
    mixed = jnp.dot(normed, joint_mat, preferred_element_type=jnp.float32)
    split = mixed.reshape(-1, 3, HEADS, HEAD_DIM)
    queries = layer_norm(split[:, 0], gains_wide[:, 2].reshape(HEADS, HEAD_DIM)).astype(
        jnp.bfloat16
    )
    keys_all = layer_norm(split[:, 1], gains_wide[:, 3].reshape(HEADS, HEAD_DIM)).astype(
        jnp.bfloat16
    )
    values = split[:, 2].astype(jnp.bfloat16)
    attended_rows, peak_rows, total_rows = ([], [], [])
    row_out, row_peaks, row_totals = attend_forward(
        queries, keys_all, values, allowed_rows[0], span, scale_factor
    )
    attended_rows.append(row_out)
    peak_rows.append(row_peaks)
    total_rows.append(row_totals)
    attended = attended_rows[0].reshape(-1, HEADS * HEAD_DIM)
    middle = hidden + jnp.dot(attended, proj_mat, preferred_element_type=jnp.float32)
    normed_two = layer_norm(middle, gains_wide[:, 1]).astype(jnp.bfloat16)
    before = jnp.dot(normed_two, upper_mat, preferred_element_type=jnp.float32)
    active = gelu_tanh(before).astype(jnp.bfloat16)
    result = middle + jnp.dot(active, lower_mat, preferred_element_type=jnp.float32)
    saved = (
        hidden,
        normed,
        split,
        queries,
        keys_all,
        values,
        peak_rows,
        total_rows,
        attended,
        middle,
        normed_two,
        before,
        active,
    )
    return (result, saved)


def layer_backward(d_hidden, saved, gathered, allowed_rows, span, scale_factor):
    joint_mat, proj_mat, upper_mat, lower_mat, gain_set = gathered
    gains_wide = gain_set.astype(jnp.float32)
    (
        hidden,
        normed,
        split,
        queries,
        keys_all,
        values,
        peak_rows,
        total_rows,
        attended,
        middle,
        normed_two,
        before,
        active,
    ) = saved
    d_branch = d_hidden.astype(jnp.bfloat16)
    d_lower = jnp.einsum("nf,nd->fd", active, d_branch, preferred_element_type=jnp.float32)
    d_active = jnp.einsum("nd,fd->nf", d_branch, lower_mat, preferred_element_type=jnp.float32)
    unused_gelu, gelu_back = jax.vjp(gelu_tanh, before)
    d_before = gelu_back(d_active)[0].astype(jnp.bfloat16)
    d_upper = jnp.einsum("nd,nf->df", normed_two, d_before, preferred_element_type=jnp.float32)
    d_normed_two = jnp.einsum("nf,df->nd", d_before, upper_mat, preferred_element_type=jnp.float32)
    unused_two, norm_two_back = jax.vjp(layer_norm, middle, gains_wide[:, 1])
    d_middle_part, d_gain_two = norm_two_back(d_normed_two)
    d_middle = d_hidden + d_middle_part
    d_attn = d_middle.astype(jnp.bfloat16)
    d_proj = jnp.einsum("nd,ne->de", attended, d_attn, preferred_element_type=jnp.float32)
    d_attended = jnp.einsum(
        "ne,de->nd", d_attn, proj_mat, preferred_element_type=jnp.float32
    ).astype(jnp.bfloat16)
    d_attended = d_attended.reshape(-1, HEADS, HEAD_DIM)
    query_parts, key_parts, value_parts = ([], [], [])
    d_q_row, d_k_row, d_v_row = attend_backward(
        queries,
        keys_all,
        values,
        allowed_rows[0],
        d_attended,
        peak_rows[0],
        total_rows[0],
        span,
        scale_factor,
    )
    query_parts.append(d_q_row)
    key_parts.append(d_k_row)
    value_parts.append(d_v_row)
    d_queries = query_parts[0]
    d_keys = key_parts[0]
    d_values = value_parts[0]
    unused_query, query_back = jax.vjp(
        layer_norm, split[:, 0], gains_wide[:, 2].reshape(HEADS, HEAD_DIM)
    )
    d_q_raw, d_gain_query = query_back(d_queries)
    unused_key, key_back = jax.vjp(
        layer_norm, split[:, 1], gains_wide[:, 3].reshape(HEADS, HEAD_DIM)
    )
    d_k_raw, d_gain_key = key_back(d_keys)
    d_mixed = (
        jnp.stack([d_q_raw, d_k_raw, d_values], axis=1)
        .reshape(d_hidden.shape[0], -1)
        .astype(jnp.bfloat16)
    )
    d_joint = jnp.einsum("nd,ne->de", normed, d_mixed, preferred_element_type=jnp.float32)
    d_normed = jnp.einsum("ne,de->nd", d_mixed, joint_mat, preferred_element_type=jnp.float32)
    unused_one, norm_one_back = jax.vjp(layer_norm, hidden, gains_wide[:, 0])
    d_input_part, d_gain_one = norm_one_back(d_normed)
    d_gains = jnp.stack(
        [d_gain_one, d_gain_two, d_gain_query.reshape(-1), d_gain_key.reshape(-1)], axis=1
    )
    return (d_middle + d_input_part, (d_joint, d_proj, d_upper, d_lower, d_gains))


def local_shards(masters, layer_index):
    return tuple((weight_arr[layer_index].astype(jnp.bfloat16) for weight_arr in masters))


def per_device(
    tokens,
    cotangent,
    segments,
    keep_mask,
    qkv_weight,
    qkv_first,
    qkv_second,
    proj_weight,
    proj_first,
    proj_second,
    up_weight,
    up_first,
    up_second,
    down_weight,
    down_first,
    down_second,
    norm_gains,
    gains_first,
    gains_second,
):
    masters = (qkv_weight, proj_weight, up_weight, down_weight, norm_gains)
    firsts = (qkv_first, proj_first, up_first, down_first, gains_first)
    seconds = (qkv_second, proj_second, up_second, down_second, gains_second)
    packs, length, width = tokens.shape
    layers = qkv_weight.shape[0]
    span = min(512, length)
    scale_factor = HEAD_DIM ** (-0.5)
    allowed_rows = [allowed_pairs(segments[0], keep_mask[0])]
    hidden = tokens.reshape(-1, width).astype(jnp.float32)
    stored, held = ([], [])
    for layer_index in range(layers):
        shards = local_shards(masters, layer_index)
        gathered = (
            lax.all_gather(shards[0], "fsdp", axis=0, tiled=True),
            lax.all_gather(shards[1], "fsdp", axis=0, tiled=True),
            lax.all_gather(shards[2], "fsdp", axis=0, tiled=True),
            lax.all_gather(shards[3], "fsdp", axis=0, tiled=True),
            lax.all_gather(shards[4], "fsdp", axis=0, tiled=True),
        )
        hidden, saved = layer_forward(hidden, gathered, allowed_rows, span, scale_factor)
        stored.append(saved)
        held.append(gathered)
    output = hidden.astype(jnp.bfloat16).reshape(tokens.shape)
    d_hidden = cotangent.reshape(-1, width).astype(jnp.float32)
    layer_grads = [None] * layers
    for layer_index in reversed(range(layers)):
        shards = local_shards(masters, layer_index)
        gathered = (
            lax.all_gather(shards[0], "fsdp", axis=0, tiled=True),
            lax.all_gather(shards[1], "fsdp", axis=0, tiled=True),
            lax.all_gather(shards[2], "fsdp", axis=0, tiled=True),
            lax.all_gather(shards[3], "fsdp", axis=0, tiled=True),
            lax.all_gather(shards[4], "fsdp", axis=0, tiled=True),
        )
        d_hidden, grads = layer_backward(
            d_hidden, stored[layer_index], gathered, allowed_rows, span, scale_factor
        )
        layer_grads[layer_index] = grads
    stacked = tuple(
        (
            jnp.stack([layer_grads[layer_index][kind_index] for layer_index in range(layers)])
            for kind_index in range(5)
        )
    )
    shares = (
        lax.psum_scatter(
            stacked[0].astype(jnp.bfloat16), "fsdp", scatter_dimension=1, tiled=True
        ).astype(jnp.float32),
        lax.psum_scatter(
            stacked[1].astype(jnp.bfloat16), "fsdp", scatter_dimension=1, tiled=True
        ).astype(jnp.float32),
        lax.psum_scatter(
            stacked[2].astype(jnp.bfloat16), "fsdp", scatter_dimension=1, tiled=True
        ).astype(jnp.float32),
        lax.psum_scatter(
            stacked[3].astype(jnp.bfloat16), "fsdp", scatter_dimension=1, tiled=True
        ).astype(jnp.float32),
        lax.psum_scatter(
            stacked[4].astype(jnp.bfloat16), "fsdp", scatter_dimension=1, tiled=True
        ).astype(jnp.float32),
    )
    summed = (
        lax.psum(shares[0].astype(jnp.bfloat16), "dp").astype(jnp.float32),
        lax.psum(shares[1].astype(jnp.bfloat16), "dp").astype(jnp.float32),
        lax.psum(shares[2].astype(jnp.bfloat16), "dp").astype(jnp.float32),
        lax.psum(shares[3].astype(jnp.bfloat16), "dp").astype(jnp.float32),
        lax.psum(shares[4].astype(jnp.bfloat16), "dp").astype(jnp.float32),
    )
    corr_one = 1.0 - 0.5**STEP
    corr_two = 1.0 - 0.5**STEP
    updated = []
    for kind_index in range(5):
        grad_now = summed[kind_index]
        first_new = 0.5 * firsts[kind_index] + 0.5 * grad_now
        second_new = 0.5 * seconds[kind_index] + 0.5 * grad_now * grad_now
        rate_now = 0.5 if kind_index == 4 else D ** (-0.5)
        decay_now = 0.0 if kind_index == 4 else 0.1
        weight_old = masters[kind_index]
        weight_new = weight_old - rate_now * (
            first_new / corr_one / (jnp.sqrt(second_new / corr_two) + adam_eps)
            + decay_now * weight_old
        )
        updated.append((weight_new, first_new, second_new))
    input_grad = d_hidden.reshape(tokens.shape)
    return (
        output,
        input_grad,
        updated[0][0],
        updated[0][1],
        updated[0][2],
        updated[1][0],
        updated[1][1],
        updated[1][2],
        updated[2][0],
        updated[2][1],
        updated[2][2],
        updated[3][0],
        updated[3][1],
        updated[3][2],
        updated[4][0],
        updated[4][1],
        updated[4][2],
    )


def solution(mesh):
    placed = (
        P(("dp", "fsdp"), None, None),
        P(("dp", "fsdp"), None, None),
        P(("dp", "fsdp"), None),
        P(("dp", "fsdp"), None),
        P(None, "fsdp", None),
        P(None, "fsdp", None),
        P(None, "fsdp", None),
        P(None, "fsdp", None),
        P(None, "fsdp", None),
        P(None, "fsdp", None),
        P(None, "fsdp", None),
        P(None, "fsdp", None),
        P(None, "fsdp", None),
        P(None, "fsdp", None),
        P(None, "fsdp", None),
        P(None, "fsdp", None),
        P(None, "fsdp", None),
        P(None, "fsdp", None),
        P(None, "fsdp", None),
    )
    return jax.shard_map(
        per_device,
        mesh=mesh,
        in_specs=placed,
        out_specs=(
            P(("dp", "fsdp"), None, None),
            P(("dp", "fsdp"), None, None),
            P(None, "fsdp", None),
            P(None, "fsdp", None),
            P(None, "fsdp", None),
            P(None, "fsdp", None),
            P(None, "fsdp", None),
            P(None, "fsdp", None),
            P(None, "fsdp", None),
            P(None, "fsdp", None),
            P(None, "fsdp", None),
            P(None, "fsdp", None),
            P(None, "fsdp", None),
            P(None, "fsdp", None),
            P(None, "fsdp", None),
            P(None, "fsdp", None),
            P(None, "fsdp", None),
        ),
        check_vma=False,
    )
```

profile of v0, /device:TPU:0, one launch (start us, length us, event | category | flops | bytes accessed | tf_op | source)
XLA Modules:
  0.0 1156.6 jit_solution(5405106433137993365)
XLA Ops:
  45.8 5.8 copy.45
  51.6 9.4 fusion.234
  66.2 9.4 fusion.181
  75.6 7.8 fusion.184
  83.4 23.9 %fusion.235 = (f32[12,512]{1,0:T(8,128)S(1)}, f32[12,512,768]{2,1,0:T(8,128)}) fusion(f32[12,512,768]{2,1,0:T(8,128)} %fusion.181, pred[512,768]{1,0:T(8,128)(4,1)S(1)} %copy-done.91), kind=kOutput, calls=%fused_computation.379 | output fusion | flops 28312320 | bytes 38166528 | tf_op jit(solution)/shard_map/sub | solution.py:58
  107.3 23.4 %fusion.236 = (f32[12,512]{1,0:T(8,128)S(1)}, f32[12,512,768]{2,1,0:T(8,128)}) fusion(f32[12,512,768]{2,1,0:T(8,128)} %fusion.184, pred[512,768]{1,0:T(8,128)(4,1)S(1)} %get-tuple-element.220), kind=kOutput, calls=%fused_computation.380 | output fusion | flops 28312320 | bytes 38166528 | tf_op jit(solution)/shard_map/sub | solution.py:58
  130.7 10.6 fusion.159
  141.4 8.6 fusion.162
  156.2 11.1 fusion.51
  167.4 12.1 %fusion.238 = (f32[1024]{0:T(1024)S(1)}, f32[1024,768]{0,1:T(8,128)S(1)}) fusion(f32[1024,768]{0,1:T(8,128)S(1)} %copy-done.6, bf16[1,3072,768]{2,1,0:T(8,128)(2,1)} %all-gather.25.cloned.1.call-done, f32[1024,3072]{1,0:T(8,128)} %fusion.51), kind=kOutput, calls=%fused_computation.382 | convolution fusion | flops 4861721600 | bytes 23597056 | tf_op jit(solution)/shard_map/dot_general | solution.py:136
  181.6 7.3 fusion.87
  195.9 8.2 fusion.175
  204.2 7.9 fusion.178
  212.0 23.5 %fusion.239 = (f32[12,512]{1,0:T(8,128)S(1)}, f32[12,512,768]{2,1,0:T(8,128)}) fusion(f32[12,512,768]{2,1,0:T(8,128)} %fusion.175, pred[512,768]{1,0:T(8,128)(4,1)S(1)} %copy-done.92), kind=kOutput, calls=%fused_computation.383 | output fusion | flops 28312320 | bytes 38166528 | tf_op jit(solution)/shard_map/sub | solution.py:58
  235.5 23.6 %fusion.240 = (f32[12,512]{1,0:T(8,128)S(1)}, f32[12,512,768]{2,1,0:T(8,128)}) fusion(f32[12,512,768]{2,1,0:T(8,128)} %fusion.178, pred[512,768]{1,0:T(8,128)(4,1)S(1)} %get-tuple-element.220), kind=kOutput, calls=%fused_computation.384 | output fusion | flops 28312320 | bytes 38166528 | tf_op jit(solution)/shard_map/sub | solution.py:58
  259.1 8.5 fusion.153
  282.1 10.9 fusion.43
  293.0 15.7 %fusion.21 = bf16[1024,3072]{1,0:T(8,128)(2,1)S(1)} fusion(f32[1024,3072]{1,0:T(8,128)} %fusion.43, bf16[1,3072,768]{2,1,0:T(8,128)(2,1)} %all-gather.33.cloned.1.call-done, bf16[1,1024,768]{2,1,0:T(8,128)(2,1)} %param.36), kind=kOutput, calls=%fused_computation.45 | convolution fusion | flops 4894752768 | bytes 25165824 | tf_op jit(solution)/shard_map/nd,fd->nf/dot_general | solution.py:175
  308.7 6.1 multiply_reduce_fusion.6
  327.9 15.0 %multiply_reduce_fusion.3 = (f32[12,512]{1,0:T(8,128)S(1)}, f32[12,512,768]{2,1,0:T(8,128)}) fusion(f32[12,512,768]{2,1,0:T(8,128)} %get-tuple-element.237, f32[12,512]{1,0:T(8,128)S(1)} %copy-done.135, bf16[512,12,64]{0,2,1:T(8,128)(2,1)S(1)} %bitcast.379, bf16[1024,3,12,64]{0,3,2,1:T(8,128)(2,1)S(1)} %bitcast.359), kind=kOutput, calls=%fused_computation.11 | convolution fusion | flops 618129408 | bytes 39772160 | tf_op jit(solution)/shard_map/qhd,khd->hqk/dot_general | solution.py:92
  342.9 13.2 %multiply_convert_fusion.3 = bf16[12,512,768]{2,1,0:T(8,128)(2,1)S(1)} fusion(f32[12,512,768]{2,1,0:T(8,128)} %get-tuple-element.242, f32[12,512]{1,0:T(8,128)S(1)} %get-tuple-element.241, f32[12,512,768]{2,1,0:T(8,128)} %get-tuple-element.237, f32[12,512]{1,0:T(8,128)S(1)} %copy-done.135), kind=kLoop, calls=%fused_computation.10 | loop fusion | flops 18874368 | bytes 47235072 | tf_op jit(solution)/shard_map/convert_element_type | solution.py:99
  362.9 15.1 %multiply_reduce_fusion.2 = (f32[12,512]{1,0:T(8,128)S(1)}, f32[12,512,768]{2,1,0:T(8,128)}) fusion(f32[12,512,768]{2,1,0:T(8,128)} %get-tuple-element.235, f32[12,512]{1,0:T(8,128)S(1)} %copy-done.133, bf16[512,12,64]{0,2,1:T(8,128)(2,1)S(1)} %bitcast.376, bf16[1024,3,12,64]{0,3,2,1:T(8,128)(2,1)S(1)} %bitcast.359), kind=kOutput, calls=%fused_computation.9 | convolution fusion | flops 618129408 | bytes 39772160 | tf_op jit(solution)/shard_map/qhd,khd->hqk/dot_general | solution.py:92
  378.0 8.4 fusion.107
  387.6 12.8 %multiply_convert_fusion.2 = bf16[12,512,768]{2,1,0:T(8,128)(2,1)S(1)} fusion(f32[12,512,768]{2,1,0:T(8,128)} %get-tuple-element.244, f32[12,512]{1,0:T(8,128)S(1)} %get-tuple-element.243, f32[12,512,768]{2,1,0:T(8,128)} %get-tuple-element.235, f32[12,512]{1,0:T(8,128)S(1)} %copy-done.133), kind=kLoop, calls=%fused_computation.8 | loop fusion | flops 18874368 | bytes 47235072 | tf_op jit(solution)/shard_map/convert_element_type | solution.py:99
  430.3 18.2 %fusion.14 = bf16[1024,3072]{1,0:T(8,128)(2,1)} fusion(f32[1024,3072]{1,0:T(8,128)} %fusion.51, bf16[1,3072,768]{2,1,0:T(8,128)(2,1)S(1)} %bitcast.384, f32[1024,768]{0,1:T(8,128)S(1)} %add_add_fusion.11), kind=kOutput, calls=%fused_computation.38 | convolution fusion | flops 4895539200 | bytes 26738688 | tf_op jit(solution)/shard_map/nd,fd->nf/dot_general | solution.py:175
  448.6 8.3 multiply_reduce_fusion.10
  469.8 12.2 %multiply_reduce_fusion.1 = (f32[12,512]{1,0:T(8,128)S(1)}, f32[12,512,768]{2,1,0:T(8,128)}) fusion(f32[12,512,768]{2,1,0:T(8,128)} %get-tuple-element.229, f32[12,512]{1,0:T(8,128)S(1)} %copy-done.131, bf16[512,12,64]{0,2,1:T(8,128)(2,1)S(1)} %bitcast.381, bf16[1024,3,12,64]{0,3,2,1:T(8,128)(2,1)} %get-tuple-element.224), kind=kOutput, calls=%fused_computation.7 | convolution fusion | flops 618129408 | bytes 39763968 | tf_op jit(solution)/shard_map/qhd,khd->hqk/dot_general | solution.py:92
  482.1 12.8 %multiply_convert_fusion.1 = bf16[12,512,768]{2,1,0:T(8,128)(2,1)S(1)} fusion(f32[12,512,768]{2,1,0:T(8,128)} %get-tuple-element.249, f32[12,512]{1,0:T(8,128)S(1)} %get-tuple-element.248, f32[12,512,768]{2,1,0:T(8,128)} %get-tuple-element.229, f32[12,512]{1,0:T(8,128)S(1)} %copy-done.131), kind=kLoop, calls=%fused_computation.6 | loop fusion | flops 18874368 | bytes 47235072 | tf_op jit(solution)/shard_map/convert_element_type | solution.py:99
  505.7 15.2 %multiply_reduce_fusion = (f32[12,512]{1,0:T(8,128)S(1)}, f32[12,512,768]{2,1,0:T(8,128)}) fusion(f32[12,512,768]{2,1,0:T(8,128)} %get-tuple-element.227, f32[12,512]{1,0:T(8,128)S(1)} %copy-done.129, bf16[512,12,64]{0,2,1:T(8,128)(2,1)S(1)} %bitcast.374, bf16[1024,3,12,64]{0,3,2,1:T(8,128)(2,1)} %get-tuple-element.224), kind=kOutput, calls=%fused_computation.5 | convolution fusion | flops 618129408 | bytes 39763968 | tf_op jit(solution)/shard_map/qhd,khd->hqk/dot_general | solution.py:92
  520.9 16.5 %multiply_convert_fusion = bf16[12,512,768]{2,1,0:T(8,128)(2,1)} fusion(f32[12,512,768]{2,1,0:T(8,128)} %get-tuple-element.251, f32[12,512]{1,0:T(8,128)S(1)} %get-tuple-element.250, f32[12,512,768]{2,1,0:T(8,128)} %get-tuple-element.227, f32[12,512]{1,0:T(8,128)S(1)} %copy-done.129), kind=kLoop, calls=%fused_computation.4 | loop fusion | flops 18874368 | bytes 47235072 | tf_op jit(solution)/shard_map/convert_element_type | solution.py:99
  537.5 6.8 convolution_multiply_fusion
  556.7 8.0 fusion.110
  578.8 13.8 %fusion.73 = bf16[1,3072,768]{2,1,0:T(8,128)(2,1)} fusion(f32[1024,768]{0,1:T(8,128)} %copy-done.13, f32[1024,3072]{1,0:T(8,128)} %fusion.51), kind=kOutput, calls=%fused_computation.132 | convolution fusion | flops 4863295488 | bytes 20447232 | tf_op jit(solution)/shard_map/nf,nd->fd/dot_general | solution.py:174
  592.6 11.9 %fusion.74 = bf16[1,3072,768]{2,1,0:T(8,128)(2,1)} fusion(bf16[1,1024,768]{2,1,0:T(8,128)(2,1)S(1)} %copy-done.53, f32[1024,3072]{1,0:T(8,128)} %fusion.43), kind=kOutput, calls=%fused_computation.133 | convolution fusion | flops 4862509056 | bytes 18874368 | tf_op jit(solution)/shard_map/nf,nd->fd/dot_general | solution.py:174
  604.5 8.4 pad_maximum_fusion.1
  613.6 10.3 fusion.72
  623.9 11.2 fusion.71
  635.1 8.4 pad_maximum_fusion
  644.5 6.8 fusion.92
  655.9 7.2 reduce-scatter.12.cloned.1.call-done
  663.1 11.0 fusion.136
  675.7 7.1 add_bitcast_fusion
  687.7 45.7 %psum.39 = bf16[2,384,4]{1,2,0:T(4,128)(2,1)S(1)} all-reduce(bf16[2,384,4]{1,2,0:T(4,128)(2,1)S(1)} %copy.57), channel_id=1, replica_groups=mesh['dp'=16,'fsdp'=2] {'dp'}, use_global_device_ids=true, to_apply=%region_61.62 | all-reduce | flops 3072 | bytes 12288 | tf_op jit(solution)/shard_map/psum | solution.py:321
  734.0 346.8 %all-reduce.7.cloned.1.call-done = (bf16[2,384,2304]{2,1,0:T(8,128)(2,1)}, bf16[2,384,768]{2,1,0:T(8,128)(2,1)}, bf16[2,384,3072]{2,1,0:T(8,128)(2,1)}, bf16[2,1536,768]{2,1,0:T(8,128)(2,1)}) async-done(((bf16[2,384,2304]{2,1,0:T(8,128)(2,1)}, bf16[2,384,768]{2,1,0:T(8,128)(2,1)}, bf16[2,384,3072]{2,1,0:T(8,128)(2,1)}, bf16[2,1536,768]{2,1,0:T(8,128)(2,1)}), (bf16[2,384,2304]{2,1,0:T(8,128)(2,1)}, ...) | async-done | bytes 14155792 | tf_op jit(solution)/shard_map/psum | solution.py:317
  1080.8 6.9 multiply_subtract_fusion.3
  1087.7 18.0 %multiply_subtract_fusion.2 = (f32[2,384,2304]{2,1,0:T(8,128)}, f32[2,384,2304]{2,1,0:T(8,128)}, f32[2,384,2304]{2,1,0:T(8,128)}) fusion(f32[2,384,2304]{2,1,0:T(8,128)} %param.39, bf16[2,384,2304]{2,1,0:T(8,128)(2,1)} %get-tuple-element.181, f32[2,384,2304]{2,1,0:T(8,128)} %param.40, f32[2,384,2304]{2,1,0:T(8,128)} %param.41), kind=kLoop, calls=%fused_computation.75 | loop fusion | flops 26542080 | bytes 46006272 | tf_op jit(solution)/shard_map/sub | solution.py:333
  1105.7 20.7 %multiply_subtract_fusion.1 = (f32[2,384,3072]{2,1,0:T(8,128)}, f32[2,384,3072]{2,1,0:T(8,128)}, f32[2,384,3072]{2,1,0:T(8,128)}) fusion(f32[2,384,3072]{2,1,0:T(8,128)S(1)} %bitcast.339, bf16[2,384,3072]{2,1,0:T(8,128)(2,1)} %get-tuple-element.183, f32[2,384,3072]{2,1,0:T(8,128)} %param.46, f32[2,384,3072]{2,1,0:T(8,128)} %param.47), kind=kLoop, calls=%fused_computation.56 | loop fusion | flops 35389440 | bytes 61341696 | tf_op jit(solution)/shard_map/sub | solution.py:333
  1126.4 23.4 %multiply_subtract_fusion = (f32[2,1536,768]{2,1,0:T(8,128)}, f32[2,1536,768]{2,1,0:T(8,128)}, f32[2,1536,768]{2,1,0:T(8,128)}) fusion(f32[2,1536,768]{2,1,0:T(8,128)} %param.48, bf16[2,1536,768]{2,1,0:T(8,128)(2,1)} %get-tuple-element.184, f32[2,1536,768]{2,1,0:T(8,128)} %param.49, f32[2,1536,768]{2,1,0:T(8,128)} %param.50), kind=kLoop, calls=%fused_computation.55 | loop fusion | flops 35389440 | bytes 61341696 | tf_op jit(solution)/shard_map/sub | solution.py:333
  (542 shorter events, 186.3 us)
Async XLA Ops:
  7.2 38.6 %all-gather.19.cloned.1.call-start = ((), (), s32[]{:S(2)}) async-start(), calls=%async_computation.9 | async-start | bytes 5308416 | tf_op jit(solution)/shard_map/all_gather | solution.py:268
  12.6 137.5 %all-gather.21.cloned.1.call-start = ((), (), s32[]{:S(2)}) async-start(), calls=%async_computation.10 | async-start | bytes 1769472 | tf_op jit(solution)/shard_map/all_gather | solution.py:269
  14.6 141.6 %all-gather.23.cloned.1.call-start = ((), (), s32[]{:S(2)}) async-start(), calls=%async_computation.11 | async-start | bytes 7077888 | tf_op jit(solution)/shard_map/all_gather | solution.py:270
  21.6 145.8 %all-gather.25.cloned.1.call-start = ((), (), s32[]{:S(2)}) async-start(), calls=%async_computation.12 | async-start | bytes 7077888 | tf_op jit(solution)/shard_map/all_gather | solution.py:271
  29.6 152.0 %all-gather.27.cloned.1.call-start = ((), (), s32[]{:S(2)}) async-start(), calls=%async_computation.13 | async-start | bytes 5308416 | tf_op jit(solution)/shard_map/all_gather | solution.py:268
  30.2 247.0 %all-gather.29.cloned.1.call-start = ((), (), s32[]{:S(2)}) async-start(), calls=%async_computation.14 | async-start | bytes 1769472 | tf_op jit(solution)/shard_map/all_gather | solution.py:269
  30.7 251.1 %all-gather.31.cloned.1.call-start = ((), (), s32[]{:S(2)}) async-start(), calls=%async_computation.15 | async-start | bytes 7077888 | tf_op jit(solution)/shard_map/all_gather | solution.py:270
  31.5 261.4 %all-gather.33.cloned.1.call-start = ((), (), s32[]{:S(2)}) async-start(), calls=%async_computation.16 | async-start | bytes 7077888 | tf_op jit(solution)/shard_map/all_gather | solution.py:271
  32.3 623.6 %reduce-scatter.10.cloned.1.call-start = ((), (), s32[]{:S(2)}) async-start(), calls=%async_computation.6 | async-start | bytes 3538944 | tf_op jit(solution)/shard_map/reduce_scatter | solution.py:303
  37.8 13.8 %copy-start.116 = (f32[768]{0:T(1024)}, f32[768]{0:T(1024)S(1)}, u32[]{:S(2)}) copy-start(f32[768]{0:T(1024)S(1)} %get-tuple-element.180) | copy-start | bytes 9220
  37.8 118.4 %copy-start.83 = (f32[768]{0:T(1024)}, f32[768]{0:T(1024)S(1)}, u32[]{:S(2)}) copy-start(f32[768]{0:T(1024)S(1)} %get-tuple-element.177) | copy-start | bytes 9220
  42.2 108.0 %copy-start.2 = (bf16[1,1024,768]{1,2,0:T(8,128)(2,1)}, bf16[1,1024,768]{1,2,0:T(8,128)(2,1)S(1)}, u32[]{:S(2)}) copy-start(bf16[1,1024,768]{1,2,0:T(8,128)(2,1)S(1)} %copy.44) | copy-start | bytes 4718596
  107.3 23.4 %copy-start.128 = (f32[12,512]{1,0:T(8,128)}, f32[12,512]{1,0:T(8,128)S(1)}, u32[]{:S(2)}) copy-start(f32[12,512]{1,0:T(8,128)S(1)} %get-tuple-element.226) | copy-start | bytes 73732
  153.6 13.8 %copy-start.76 = (f32[1024]{0:T(1024)}, f32[1024]{0:T(1024)S(1)}, u32[]{:S(2)}) copy-start(f32[1024]{0:T(1024)S(1)} %broadcast_multiply_fusion.6) | copy-start | bytes 12292
  235.5 23.6 %copy-start.132 = (f32[12,512]{1,0:T(8,128)}, f32[12,512]{1,0:T(8,128)S(1)}, u32[]{:S(2)}) copy-start(f32[12,512]{1,0:T(8,128)S(1)} %get-tuple-element.234) | copy-start | bytes 73732
  259.1 12.1 %copy-start.27 = (f32[12,512,768]{2,1,0:T(8,128)S(1)}, f32[12,512,768]{2,1,0:T(8,128)}, u32[]{:S(2)}) copy-start(f32[12,512,768]{2,1,0:T(8,128)} %get-tuple-element.237) | copy-start | bytes 56623108
  281.4 33.5 %copy-start.4 = (f32[1024,768]{0,1:T(8,128)}, f32[1024,768]{0,1:T(8,128)S(1)}, u32[]{:S(2)}) copy-start(f32[1024,768]{0,1:T(8,128)S(1)} %get-tuple-element.239) | copy-start | bytes 9437188
  281.4 33.4 %copy-start.79 = (f32[1024]{0:T(1024)}, f32[1024]{0:T(1024)S(1)}, u32[]{:S(2)}) copy-start(f32[1024]{0:T(1024)S(1)} %broadcast_multiply_fusion.4) | copy-start | bytes 12292
  281.8 33.0 %copy-start.89 = (f32[1024]{0:T(1024)}, f32[1024]{0:T(1024)S(1)}, u32[]{:S(2)}) copy-start(f32[1024]{0:T(1024)S(1)} %fusion.209) | copy-start | bytes 12292
  293.0 15.7 %copy-start.38 = (bf16[1,768,3072]{2,1,0:T(8,128)(2,1)S(1)}, bf16[1,768,3072]{2,1,0:T(8,128)(2,1)}, u32[]{:S(2)}) copy-start(bf16[1,768,3072]{2,1,0:T(8,128)(2,1)} %all-gather.31.cloned.1.call-done) | copy-start | bytes 14155780
  342.9 13.2 %copy-start.19 = (bf16[1024,12,64]{0,2,1:T(8,128)(2,1)S(1)}, bf16[1024,12,64]{0,2,1:T(8,128)(2,1)}, u32[]{:S(2)}) copy-start(bf16[1024,12,64]{0,2,1:T(8,128)(2,1)} %copy-done.18) | copy-start | bytes 4718596
  378.0 26.5 %slice-start = ((s8[9437184]{0:T(1024)(128)(4,1)}), s8[4194304]{0:T(1024)(128)(4,1)S(1)}, s32[]{:S(2)}) async-start(s8[9437184]{0:T(1024)(128)(4,1)} %bitcast.327), calls=%async_computation.19 | async-start | bytes 8388608
  378.0 26.5 %slice-start.1 = ((s8[9437184]{0:T(1024)(128)(4,1)}), s8[4194304]{0:T(1024)(128)(4,1)S(1)}, s32[]{:S(2)}) async-start(s8[9437184]{0:T(1024)(128)(4,1)} %bitcast.327), calls=%async_computation.20 | async-start | bytes 8388608
  387.6 16.9 %slice-start.2 = ((s8[9437184]{0:T(1024)(128)(4,1)}), s8[1048576]{0:T(1024)(128)(4,1)S(1)}, s32[]{:S(2)}) async-start(s8[9437184]{0:T(1024)(128)(4,1)} %bitcast.327), calls=%async_computation.21 | async-start | bytes 2097152
  428.7 19.8 %slice-start.22 = ((s8[4718592]{0:T(1024)(128)(4,1)}), s8[4194304]{0:T(1024)(128)(4,1)S(1)}, s32[]{:S(2)}) async-start(s8[4718592]{0:T(1024)(128)(4,1)} %bitcast.356), calls=%async_computation.41 | async-start | bytes 8388608
  430.2 27.5 %copy-start.13 = (f32[1024,768]{0,1:T(8,128)}, f32[1024,768]{0,1:T(8,128)S(1)}, u32[]{:S(2)}) copy-start(f32[1024,768]{0,1:T(8,128)S(1)} %add_add_fusion.11) | copy-start | bytes 9437188
  430.2 18.3 %copy-start.7 = (f32[1024,768]{0,1:T(8,128)S(1)}, f32[1024,768]{0,1:T(8,128)}, u32[]{:S(2)}) copy-start(f32[1024,768]{0,1:T(8,128)} %copy-done.5) | copy-start | bytes 9437188
  430.3 18.3 %slice-start.23 = ((s8[4718592]{0:T(1024)(128)(4,1)}), s8[524288]{0:T(1024)(128)(4,1)S(1)}, s32[]{:S(2)}) async-start(s8[4718592]{0:T(1024)(128)(4,1)} %bitcast.356), calls=%async_computation.42 | async-start | bytes 1048576
  430.3 18.3 %copy-start.77 = (f32[1024]{0:T(1024)S(1)}, f32[1024]{0:T(1024)}, u32[]{:S(2)}) copy-start(f32[1024]{0:T(1024)} %copy-done.76) | copy-start | bytes 12292
  430.3 18.3 %copy-start.84 = (f32[768]{0:T(1024)S(1)}, f32[768]{0:T(1024)}, u32[]{:S(2)}) copy-start(f32[768]{0:T(1024)} %copy-done.83) | copy-start | bytes 9220
  430.3 18.3 %copy-start.87 = (f32[1024]{0:T(1024)S(1)}, f32[1024]{0:T(1024)}, u32[]{:S(2)}) copy-start(f32[1024]{0:T(1024)} %copy-done.86) | copy-start | bytes 12292
  482.1 12.8 %copy-start.17 = (bf16[1024,12,64]{0,2,1:T(8,128)(2,1)S(1)}, bf16[1024,12,64]{0,2,1:T(8,128)(2,1)}, u32[]{:S(2)}) copy-start(bf16[1024,12,64]{0,2,1:T(8,128)(2,1)} %copy-done.16) | copy-start | bytes 4718596
  502.6 153.3 %reduce-scatter.8.cloned.1.call-start = ((), (), s32[]{:S(2)}) async-start(), calls=%async_computation.5 | async-start | bytes 10616832 | tf_op jit(solution)/shard_map/reduce_scatter | solution.py:300
  505.7 38.5 %slice-start.3 = ((s8[9437184]{0:T(1024)(128)(4,1)}), s8[4194304]{0:T(1024)(128)(4,1)S(1)}, s32[]{:S(2)}) async-start(s8[9437184]{0:T(1024)(128)(4,1)} %bitcast.334), calls=%async_computation.22 | async-start | bytes 8388608
  505.7 38.5 %slice-start.4 = ((s8[9437184]{0:T(1024)(128)(4,1)}), s8[1048576]{0:T(1024)(128)(4,1)S(1)}, s32[]{:S(2)}) async-start(s8[9437184]{0:T(1024)(128)(4,1)} %bitcast.334), calls=%async_computation.23 | async-start | bytes 2097152
  520.9 23.4 %slice-start.5 = ((s8[9437184]{0:T(1024)(128)(4,1)}), s8[4194304]{0:T(1024)(128)(4,1)S(1)}, s32[]{:S(2)}) async-start(s8[9437184]{0:T(1024)(128)(4,1)} %bitcast.334), calls=%async_computation.24 | async-start | bytes 8388608
  578.7 13.9 %copy-start.53 = (bf16[1,1024,768]{2,1,0:T(8,128)(2,1)S(1)}, bf16[1,1024,768]{2,1,0:T(8,128)(2,1)}, u32[]{:S(2)}) copy-start(bf16[1,1024,768]{2,1,0:T(8,128)(2,1)} %param.36) | copy-start | bytes 4718596
  578.7 77.2 %reduce-scatter.14.cloned.1.call-start = ((), (), s32[]{:S(2)}) async-start(), calls=%async_computation.8 | async-start | bytes 14155776 | tf_op jit(solution)/shard_map/reduce_scatter | solution.py:309
  613.0 50.1 %reduce-scatter.12.cloned.1.call-start = ((), (), s32[]{:S(2)}) async-start(), calls=%async_computation.7 | async-start | bytes 14155776 | tf_op jit(solution)/shard_map/reduce_scatter | solution.py:306
  643.5 43.0 %reduce-scatter.16.cloned.1.call-start = ((), (), s32[]{:S(2)}) async-start(), calls=%async_computation.17 | async-start | bytes 294912
  655.8 425.0 %all-reduce.7.cloned.1.call-start = ((), (), s32[]{:S(2)}) async-start(), calls=%async_computation.18 | async-start | bytes 28311552 | tf_op jit(solution)/shard_map/psum | solution.py:317
  682.8 50.5 %copy-start.107 = (f32[2,384,4]{1,2,0:T(4,128)S(1)}, f32[2,384,4]{1,2,0:T(4,128)}, u32[]{:S(2)}) copy-start(f32[2,384,4]{1,2,0:T(4,128)} %param.51) | copy-start | bytes 36868
  682.8 50.6 %copy-start.139 = (f32[2,384,4]{1,2,0:T(4,128)S(1)}, f32[2,384,4]{1,2,0:T(4,128)}, u32[]{:S(2)}) copy-start(f32[2,384,4]{1,2,0:T(4,128)} %param.52) | copy-start | bytes 36868
  682.8 50.6 %copy-start.140 = (f32[2,384,4]{1,2,0:T(4,128)S(1)}, f32[2,384,4]{1,2,0:T(4,128)}, u32[]{:S(2)}) copy-start(f32[2,384,4]{1,2,0:T(4,128)} %param.53) | copy-start | bytes 36868
  682.8 398.0 %copy-start.34 = (f32[2,384,768]{2,1,0:T(8,128)S(1)}, f32[2,384,768]{2,1,0:T(8,128)}, u32[]{:S(2)}) copy-start(f32[2,384,768]{2,1,0:T(8,128)} %param.42) | copy-start | bytes 7077892
  1080.8 24.9 %slice-start.9 = ((s8[9437184]{0:T(1024)(128)(4,1)}), s8[4194304]{0:T(1024)(128)(4,1)S(1)}, s32[]{:S(2)}) async-start(s8[9437184]{0:T(1024)(128)(4,1)} %bitcast.338), calls=%async_computation.28 | async-start | bytes 8388608
  1087.7 18.0 %slice-start.10 = ((s8[9437184]{0:T(1024)(128)(4,1)}), s8[4194304]{0:T(1024)(128)(4,1)S(1)}, s32[]{:S(2)}) async-start(s8[9437184]{0:T(1024)(128)(4,1)} %bitcast.338), calls=%async_computation.29 | async-start | bytes 8388608
  1087.7 18.0 %slice-start.11 = ((s8[9437184]{0:T(1024)(128)(4,1)}), s8[1048576]{0:T(1024)(128)(4,1)S(1)}, s32[]{:S(2)}) async-start(s8[9437184]{0:T(1024)(128)(4,1)} %bitcast.338), calls=%async_computation.30 | async-start | bytes 2097152
  (145 other events, 582.6 us)
Sparse Core Ops, SparseCore 0:
  12.8 15.3 all-gather.18
  30.3 10.3 all-gather.20
  42.9 15.5 all-gather.22
  60.5 15.5 all-gather.24
  78.1 13.8 all-gather.26
  94.0 10.3 all-gather.28
  106.5 15.5 all-gather.30
  124.3 15.5 all-gather.32
  502.7 11.6 reduce-scatter.9
  578.8 17.2 reduce-scatter.7
  613.1 19.5 reduce-scatter.13
  643.6 19.4 reduce-scatter.11
  665.9 8.8 reduce-scatter.15
  681.1 399.6 all-reduce.6
where the time goes:
time: 1160 us
  matrix products  364 us (31%)
  waiting for transfers between devices  357 us (31%)
  other arithmetic  302 us (26%)
  local copies, waits for them, and re-layouts  66.4 us (6%)
  blocking collectives  49.7 us (4%)
  between operations  16.6 us (1%)
    psum x1, waiting for transfers between devices, per_device(): lax.psum(shares[0].astype(jnp.bfloat16), 'dp').astype(jnp.float32)  347 us
    sub x4, other arithmetic, attend_forward(): expo = jnp.exp(masked - peak)  94.3 us
    sub x5, other arithmetic, per_device(): weight_old - rate_now * (first_new / corr_one / (jnp.sqrt(second_new / co...  69.6 us
    dot_general x4, matrix products, attend_backward(): jnp.einsum('qhd,khd->hqk', d_block, values_part, preferred_element_type=j...  57.5 us
    convert_element_type x4, other arithmetic, attend_backward(): d_scores = (probs_raw * (d_probs - inner)).astype(jnp.bfloat16)  55.3 us
    psum x1, blocking collectives, per_device(): lax.psum(shares[4].astype(jnp.bfloat16), 'dp').astype(jnp.float32)  45.7 us
    unnamed x366, local copies, waits for them, and re-layouts  42.8 us
    dot_general x2, matrix products, layer_backward(): jnp.einsum('nd,fd->nf', d_branch, lower_mat, preferred_element_type=jnp.f...  33.9 us
  transfers between devices with their start and end apart: 14, of which 2 were waited for; matrix products, arithmetic and copies ran while one was open for 37% of the time, Pallas kernels for 0%

commit v1 on v0

--- a/solution.py
+++ b/solution.py
@@ -314,7 +314,7 @@
         ).astype(jnp.float32),
     )
     summed = (
-        lax.psum(shares[0].astype(jnp.bfloat16), "dp").astype(jnp.float32),
+        jnp.sum(lax.all_gather(shares[0].astype(jnp.bfloat16), "dp"), axis=0).astype(jnp.float32),
         lax.psum(shares[1].astype(jnp.bfloat16), "dp").astype(jnp.float32),
         lax.psum(shares[2].astype(jnp.bfloat16), "dp").astype(jnp.float32),
         lax.psum(shares[3].astype(jnp.bfloat16), "dp").astype(jnp.float32),

time: 1160 us -> 1620 us (1.40)
  waiting for transfers between devices: 357 us -> 788 us
  other arithmetic: 302 us -> 325 us
    all_gather x0 -> x1, waiting for transfers between devices: none -> 518 us  [per_device(): lax.all_gather(shares[0].astype(jnp.bfloat16), 'dp')]
    psum x1, waiting for transfers between devices: 347 us -> 262 us  [per_device(): lax.psum(shares[1].astype(jnp.bfloat16), 'dp').astype(jnp.float32)]
    reduce_sum x0 -> x1, other arithmetic: none -> 19 us  [per_device(): jnp.sum(lax.all_gather(shares[0].astype(jnp.bfloat16), 'dp'), axis=0)]
    unnamed x366 -> x350, local copies, waits for them, and re-layouts: 42.8 us -> 44 us
  transfers between devices with their start and end apart: 14 -> 15, of which waited for: 2 -> 3; matrix products, arithmetic and copies ran while one was open for 37% -> 33% of each run, Pallas kernels for 0% -> 0%
where the time goes in v1:
time: 1620 us; the launch traced here: 1610 us
  waiting for transfers between devices  788 us (49%)
  matrix products  368 us (23%)
  other arithmetic  325 us (20%)
  local copies, waits for them, and re-layouts  66.1 us (4%)
  blocking collectives  49.7 us (3%)
  between operations  16.5 us (1%)
    all_gather x1, waiting for transfers between devices, per_device(): lax.all_gather(shares[0].astype(jnp.bfloat16), 'dp')  518 us
    psum x1, waiting for transfers between devices, per_device(): lax.psum(shares[1].astype(jnp.bfloat16), 'dp').astype(jnp.float32)  262 us
    sub x4, other arithmetic, attend_forward(): expo = jnp.exp(masked - peak)  94.4 us
    sub x5, other arithmetic, per_device(): weight_old - rate_now * (first_new / corr_one / (jnp.sqrt(second_new / co...  69.3 us
    convert_element_type x4, other arithmetic, attend_backward(): d_scores = (probs_raw * (d_probs - inner)).astype(jnp.bfloat16)  58.2 us
    dot_general x4, matrix products, attend_backward(): jnp.einsum('qhd,khd->hqk', d_block, values_part, preferred_element_type=j...  55.9 us
    psum x1, blocking collectives, per_device(): lax.psum(shares[4].astype(jnp.bfloat16), 'dp').astype(jnp.float32)  45.6 us
    unnamed x350, local copies, waits for them, and re-layouts  44 us
  transfers between devices with their start and end apart: 15, of which 3 were waited for; matrix products, arithmetic and copies ran while one was open for 33% of the time, Pallas kernels for 0%

profile of v1, /device:TPU:0, one launch (start us, length us, event | category | flops | bytes accessed | tf_op | source)
XLA Modules:
  0.0 1614.3 jit_solution(14598329960546203916)
XLA Ops:
  51.6 9.4 fusion.234
  66.2 9.4 fusion.181
  75.7 7.8 fusion.184
  83.5 23.9 %fusion.235 = (f32[12,512]{1,0:T(8,128)S(1)}, f32[12,512,768]{2,1,0:T(8,128)}) fusion(f32[12,512,768]{2,1,0:T(8,128)} %fusion.181, pred[512,768]{1,0:T(8,128)(4,1)S(1)} %copy-done.90), kind=kOutput, calls=%fused_computation.379 | output fusion | flops 28312320 | bytes 38166528 | tf_op jit(solution)/shard_map/sub | solution.py:58
  107.4 23.5 %fusion.236 = (f32[12,512]{1,0:T(8,128)S(1)}, f32[12,512,768]{2,1,0:T(8,128)}) fusion(f32[12,512,768]{2,1,0:T(8,128)} %fusion.184, pred[512,768]{1,0:T(8,128)(4,1)S(1)} %get-tuple-element.219), kind=kOutput, calls=%fused_computation.380 | output fusion | flops 28312320 | bytes 38166528 | tf_op jit(solution)/shard_map/sub | solution.py:58
  130.8 10.6 fusion.159
  141.5 8.6 fusion.162
  156.3 11.1 fusion.51
  167.5 12.1 fusion.238
  181.7 7.3 fusion.87
  196.1 8.2 fusion.175
  204.3 7.9 fusion.178
  212.2 23.3 %fusion.239 = (f32[12,512]{1,0:T(8,128)S(1)}, f32[12,512,768]{2,1,0:T(8,128)}) fusion(f32[12,512,768]{2,1,0:T(8,128)} %fusion.175, pred[512,768]{1,0:T(8,128)(4,1)S(1)} %copy-done.91), kind=kOutput, calls=%fused_computation.383 | output fusion | flops 28312320 | bytes 38166528 | tf_op jit(solution)/shard_map/sub | solution.py:58
  235.5 23.7 %fusion.240 = (f32[12,512]{1,0:T(8,128)S(1)}, f32[12,512,768]{2,1,0:T(8,128)}) fusion(f32[12,512,768]{2,1,0:T(8,128)} %fusion.178, pred[512,768]{1,0:T(8,128)(4,1)S(1)} %get-tuple-element.219), kind=kOutput, calls=%fused_computation.384 | output fusion | flops 28312320 | bytes 38166528 | tf_op jit(solution)/shard_map/sub | solution.py:58
  259.2 8.5 fusion.153
  282.2 10.9 fusion.43
  293.1 15.7 fusion.21
  328.0 15.1 multiply_reduce_fusion.3
  343.1 13.2 multiply_convert_fusion.3
  363.1 15.1 multiply_reduce_fusion.2
  378.2 8.4 fusion.107
  387.8 12.8 multiply_convert_fusion.2
  430.5 17.9 %fusion.14 = bf16[1024,3072]{1,0:T(8,128)(2,1)} fusion(f32[1024,3072]{1,0:T(8,128)} %fusion.51, bf16[1,3072,768]{2,1,0:T(8,128)(2,1)S(1)} %bitcast.382, f32[1024,768]{0,1:T(8,128)S(1)} %add_add_fusion.11), kind=kOutput, calls=%fused_computation.38 | convolution fusion | flops 4895539200 | bytes 26738688 | tf_op jit(solution)/shard_map/nd,fd->nf/dot_general | solution.py:175
  448.4 8.3 multiply_reduce_fusion.10
  463.7 14.1 fusion.73
  477.8 11.6 fusion.74
  489.4 8.4 pad_maximum_fusion.1
  503.5 11.3 fusion.72
  514.8 6.8 fusion.71
  521.6 8.4 pad_maximum_fusion
  530.0 12.3 multiply_reduce_fusion.1
  542.4 15.7 multiply_convert_fusion.1
  560.2 7.8 fusion.115
  575.5 13.5 multiply_reduce_fusion
  589.0 16.6 %multiply_convert_fusion = bf16[12,512,768]{2,1,0:T(8,128)(2,1)} fusion(f32[12,512,768]{2,1,0:T(8,128)} %get-tuple-element.250, f32[12,512]{1,0:T(8,128)S(1)} %get-tuple-element.249, f32[12,512,768]{2,1,0:T(8,128)} %get-tuple-element.226, f32[12,512]{1,0:T(8,128)S(1)} %copy-done.128), kind=kLoop, calls=%fused_computation.4 | loop fusion | flops 18874368 | bytes 47235072 | tf_op jit(solution)/shard_map/convert_element_type | solution.py:99
  605.6 6.7 convolution_multiply_fusion
  627.2 7.8 fusion.110
  649.8 6.8 fusion.92
  667.0 11.2 fusion.136
  679.8 7.1 add_bitcast_fusion
  693.5 45.6 %psum.31 = bf16[2,384,4]{1,2,0:T(4,128)(2,1)S(1)} all-reduce(bf16[2,384,4]{1,2,0:T(4,128)(2,1)S(1)} %copy.57), channel_id=1, replica_groups=mesh['dp'=16,'fsdp'=2] {'dp'}, use_global_device_ids=true, to_apply=%region_61.62 | all-reduce | flops 3072 | bytes 12288 | tf_op jit(solution)/shard_map/psum | solution.py:321
  739.8 262.4 %all-reduce.7.cloned.1.call-done = (bf16[2,384,768]{2,1,0:T(8,128)(2,1)}, bf16[2,384,3072]{2,1,0:T(8,128)(2,1)}, bf16[2,1536,768]{2,1,0:T(8,128)(2,1)}) async-done(((bf16[2,384,768]{2,1,0:T(8,128)(2,1)}, bf16[2,384,3072]{2,1,0:T(8,128)(2,1)}, bf16[2,1536,768]{2,1,0:T(8,128)(2,1)}), (bf16[2,384,768]{2,1,0:T(8,128)(2,1)}, bf16[2,384,3072]{2,1,0:T(8,128)(2,1)}, ...) | async-done | bytes 10616848 | tf_op jit(solution)/shard_map/psum | solution.py:318
  1002.2 6.9 multiply_subtract_fusion.3
  1009.2 22.7 %multiply_subtract_fusion.1 = (f32[2,384,3072]{2,1,0:T(8,128)}, f32[2,384,3072]{2,1,0:T(8,128)}, f32[2,384,3072]{2,1,0:T(8,128)}) fusion(f32[2,384,3072]{2,1,0:T(8,128)S(1)} %bitcast.339, bf16[2,384,3072]{2,1,0:T(8,128)(2,1)} %get-tuple-element.182, f32[2,384,3072]{2,1,0:T(8,128)} %param.46, f32[2,384,3072]{2,1,0:T(8,128)} %param.47), kind=kLoop, calls=%fused_computation.56 | loop fusion | flops 35389440 | bytes 61341696 | tf_op jit(solution)/shard_map/sub | solution.py:333
  1031.9 23.6 %multiply_subtract_fusion = (f32[2,1536,768]{2,1,0:T(8,128)}, f32[2,1536,768]{2,1,0:T(8,128)}, f32[2,1536,768]{2,1,0:T(8,128)}) fusion(f32[2,1536,768]{2,1,0:T(8,128)} %param.48, bf16[2,1536,768]{2,1,0:T(8,128)(2,1)} %get-tuple-element.183, f32[2,1536,768]{2,1,0:T(8,128)} %param.49, f32[2,1536,768]{2,1,0:T(8,128)} %param.50), kind=kLoop, calls=%fused_computation.55 | loop fusion | flops 35389440 | bytes 61341696 | tf_op jit(solution)/shard_map/sub | solution.py:333
  1055.5 517.6 %all-gather.37.cloned.1.call-done = bf16[32,384,2304]{2,1,0:T(8,128)(2,1)} async-done(((bf16[2,384,2304]{2,1,0:T(8,128)(2,1)}), bf16[32,384,2304]{2,1,0:T(8,128)(2,1)}) %all-gather.37.cloned.1.call-update) | async-done | bytes 56623120 | tf_op jit(solution)/shard_map/all_gather | solution.py:317
  1573.1 19.0 %reduce_sum.504 = bf16[2,384,2304]{2,1,0:T(8,128)(2,1)S(1)} reduce(bf16[16,2,384,2304]{3,2,1,0:T(8,128)(2,1)} %bitcast.337, bf16[]{:T(256)} %constant.276.clone.1), dimensions={0}, to_apply=%region_45.46 | reduce | flops 26542080 | bytes 60162048 | tf_op jit(solution)/shard_map/reduce_sum | solution.py:317
  1592.1 15.5 multiply_subtract_fusion.2
  (529 shorter events, 205.7 us)
Async XLA Ops:
  7.2 38.6 %all-gather.21.cloned.1.call-start = ((), (), s32[]{:S(2)}) async-start(), calls=%async_computation.9 | async-start | bytes 5308416 | tf_op jit(solution)/shard_map/all_gather | solution.py:268
  12.6 137.6 %all-gather.23.cloned.1.call-start = ((), (), s32[]{:S(2)}) async-start(), calls=%async_computation.10 | async-start | bytes 1769472 | tf_op jit(solution)/shard_map/all_gather | solution.py:269
  14.6 141.7 %all-gather.25.cloned.1.call-start = ((), (), s32[]{:S(2)}) async-start(), calls=%async_computation.11 | async-start | bytes 7077888 | tf_op jit(solution)/shard_map/all_gather | solution.py:270
  21.6 145.9 %all-gather.27.cloned.1.call-start = ((), (), s32[]{:S(2)}) async-start(), calls=%async_computation.12 | async-start | bytes 7077888 | tf_op jit(solution)/shard_map/all_gather | solution.py:271
  29.6 152.1 %all-gather.29.cloned.1.call-start = ((), (), s32[]{:S(2)}) async-start(), calls=%async_computation.13 | async-start | bytes 5308416 | tf_op jit(solution)/shard_map/all_gather | solution.py:268
  30.2 247.1 %all-gather.31.cloned.1.call-start = ((), (), s32[]{:S(2)}) async-start(), calls=%async_computation.14 | async-start | bytes 1769472 | tf_op jit(solution)/shard_map/all_gather | solution.py:269
  30.7 251.2 %all-gather.33.cloned.1.call-start = ((), (), s32[]{:S(2)}) async-start(), calls=%async_computation.15 | async-start | bytes 7077888 | tf_op jit(solution)/shard_map/all_gather | solution.py:270
  31.5 261.6 %all-gather.35.cloned.1.call-start = ((), (), s32[]{:S(2)}) async-start(), calls=%async_computation.16 | async-start | bytes 7077888 | tf_op jit(solution)/shard_map/all_gather | solution.py:271
  32.3 629.2 %reduce-scatter.10.cloned.1.call-start = ((), (), s32[]{:S(2)}) async-start(), calls=%async_computation.6 | async-start | bytes 3538944 | tf_op jit(solution)/shard_map/reduce_scatter | solution.py:303
  37.8 13.9 copy-start.115
  37.8 118.5 %copy-start.84 = (f32[768]{0:T(1024)}, f32[768]{0:T(1024)S(1)}, u32[]{:S(2)}) copy-start(f32[768]{0:T(1024)S(1)} %get-tuple-element.177) | copy-start | bytes 9220
  42.2 108.1 %copy-start.2 = (bf16[1,1024,768]{1,2,0:T(8,128)(2,1)}, bf16[1,1024,768]{1,2,0:T(8,128)(2,1)S(1)}, u32[]{:S(2)}) copy-start(bf16[1,1024,768]{1,2,0:T(8,128)(2,1)S(1)} %copy.44) | copy-start | bytes 4718596
  107.4 23.5 %copy-start.127 = (f32[12,512]{1,0:T(8,128)}, f32[12,512]{1,0:T(8,128)S(1)}, u32[]{:S(2)}) copy-start(f32[12,512]{1,0:T(8,128)S(1)} %get-tuple-element.225) | copy-start | bytes 73732
  153.7 13.8 copy-start.78
  235.5 23.7 %copy-start.131 = (f32[12,512]{1,0:T(8,128)}, f32[12,512]{1,0:T(8,128)S(1)}, u32[]{:S(2)}) copy-start(f32[12,512]{1,0:T(8,128)S(1)} %get-tuple-element.233) | copy-start | bytes 73732
  259.2 12.1 copy-start.28
  281.5 33.5 %copy-start.4 = (f32[1024,768]{0,1:T(8,128)}, f32[1024,768]{0,1:T(8,128)S(1)}, u32[]{:S(2)}) copy-start(f32[1024,768]{0,1:T(8,128)S(1)} %get-tuple-element.238) | copy-start | bytes 9437188
  281.5 33.4 %copy-start.80 = (f32[1024]{0:T(1024)}, f32[1024]{0:T(1024)S(1)}, u32[]{:S(2)}) copy-start(f32[1024]{0:T(1024)S(1)} %broadcast_multiply_fusion.4) | copy-start | bytes 12292
  281.9 33.0 %copy-start.88 = (f32[1024]{0:T(1024)}, f32[1024]{0:T(1024)S(1)}, u32[]{:S(2)}) copy-start(f32[1024]{0:T(1024)S(1)} %fusion.209) | copy-start | bytes 12292
  293.1 15.7 copy-start.38
  343.1 13.2 copy-start.19
  378.2 26.5 %slice-start = ((s8[9437184]{0:T(1024)(128)(4,1)}), s8[4194304]{0:T(1024)(128)(4,1)S(1)}, s32[]{:S(2)}) async-start(s8[9437184]{0:T(1024)(128)(4,1)} %bitcast.328), calls=%async_computation.20 | async-start | bytes 8388608
  378.2 26.5 %slice-start.1 = ((s8[9437184]{0:T(1024)(128)(4,1)}), s8[4194304]{0:T(1024)(128)(4,1)S(1)}, s32[]{:S(2)}) async-start(s8[9437184]{0:T(1024)(128)(4,1)} %bitcast.328), calls=%async_computation.21 | async-start | bytes 8388608
  387.8 16.9 %slice-start.2 = ((s8[9437184]{0:T(1024)(128)(4,1)}), s8[1048576]{0:T(1024)(128)(4,1)S(1)}, s32[]{:S(2)}) async-start(s8[9437184]{0:T(1024)(128)(4,1)} %bitcast.328), calls=%async_computation.22 | async-start | bytes 2097152
  428.9 19.4 %slice-start.14 = ((s8[4718592]{0:T(1024)(128)(4,1)}), s8[524288]{0:T(1024)(128)(4,1)S(1)}, s32[]{:S(2)}) async-start(s8[4718592]{0:T(1024)(128)(4,1)} %bitcast.354), calls=%async_computation.34 | async-start | bytes 1048576
  430.4 27.2 %copy-start.13 = (f32[1024,768]{0,1:T(8,128)}, f32[1024,768]{0,1:T(8,128)S(1)}, u32[]{:S(2)}) copy-start(f32[1024,768]{0,1:T(8,128)S(1)} %add_add_fusion.11) | copy-start | bytes 9437188
  430.4 17.9 %copy-start.8 = (f32[1024,768]{0,1:T(8,128)S(1)}, f32[1024,768]{0,1:T(8,128)}, u32[]{:S(2)}) copy-start(f32[1024,768]{0,1:T(8,128)} %copy-done.6) | copy-start | bytes 9437188
  430.4 17.9 %slice-start.15 = ((s8[4718592]{0:T(1024)(128)(4,1)}), s8[4194304]{0:T(1024)(128)(4,1)S(1)}, s32[]{:S(2)}) async-start(s8[4718592]{0:T(1024)(128)(4,1)} %bitcast.354), calls=%async_computation.35 | async-start | bytes 8388608
  430.5 17.9 %copy-start.79 = (f32[1024]{0:T(1024)S(1)}, f32[1024]{0:T(1024)}, u32[]{:S(2)}) copy-start(f32[1024]{0:T(1024)} %copy-done.78) | copy-start | bytes 12292
  430.5 17.9 %copy-start.85 = (f32[768]{0:T(1024)S(1)}, f32[768]{0:T(1024)}, u32[]{:S(2)}) copy-start(f32[768]{0:T(1024)} %copy-done.84) | copy-start | bytes 9220
  430.5 17.9 %copy-start.87 = (f32[1024]{0:T(1024)S(1)}, f32[1024]{0:T(1024)}, u32[]{:S(2)}) copy-start(f32[1024]{0:T(1024)} %copy-done.86) | copy-start | bytes 12292
  463.6 197.9 %reduce-scatter.14.cloned.1.call-start = ((), (), s32[]{:S(2)}) async-start(), calls=%async_computation.8 | async-start | bytes 14155776 | tf_op jit(solution)/shard_map/reduce_scatter | solution.py:309
  463.7 14.1 copy-start.55
  497.8 163.8 %reduce-scatter.12.cloned.1.call-start = ((), (), s32[]{:S(2)}) async-start(), calls=%async_computation.7 | async-start | bytes 14155776 | tf_op jit(solution)/shard_map/reduce_scatter | solution.py:306
  501.0 13.8 slice-start.22
  542.3 124.7 %reduce-scatter.8.cloned.1.call-start = ((), (), s32[]{:S(2)}) async-start(), calls=%async_computation.5 | async-start | bytes 10616832 | tf_op jit(solution)/shard_map/reduce_scatter | solution.py:300
  542.4 15.7 copy-start.23
  575.5 36.8 %slice-start.3 = ((s8[9437184]{0:T(1024)(128)(4,1)}), s8[4194304]{0:T(1024)(128)(4,1)S(1)}, s32[]{:S(2)}) async-start(s8[9437184]{0:T(1024)(128)(4,1)} %bitcast.335), calls=%async_computation.23 | async-start | bytes 8388608
  575.5 36.8 %slice-start.4 = ((s8[9437184]{0:T(1024)(128)(4,1)}), s8[1048576]{0:T(1024)(128)(4,1)S(1)}, s32[]{:S(2)}) async-start(s8[9437184]{0:T(1024)(128)(4,1)} %bitcast.335), calls=%async_computation.24 | async-start | bytes 2097152
  589.0 23.3 %slice-start.5 = ((s8[9437184]{0:T(1024)(128)(4,1)}), s8[4194304]{0:T(1024)(128)(4,1)S(1)}, s32[]{:S(2)}) async-start(s8[9437184]{0:T(1024)(128)(4,1)} %bitcast.335), calls=%async_computation.25 | async-start | bytes 8388608
  648.8 41.9 %reduce-scatter.16.cloned.1.call-start = ((), (), s32[]{:S(2)}) async-start(), calls=%async_computation.18 | async-start | bytes 294912
  661.4 340.8 %all-reduce.7.cloned.1.call-start = ((), (), s32[]{:S(2)}) async-start(), calls=%async_computation.19 | async-start | bytes 21233664 | tf_op jit(solution)/shard_map/psum | solution.py:318
  662.0 911.1 %all-gather.37.cloned.1.call-start = ((), (), s32[]{:S(2)}) async-start(), calls=%async_computation.17 | async-start | bytes 60162048 | tf_op jit(solution)/shard_map/all_gather | solution.py:317
  686.9 52.2 %copy-start.106 = (f32[2,384,4]{1,2,0:T(4,128)S(1)}, f32[2,384,4]{1,2,0:T(4,128)}, u32[]{:S(2)}) copy-start(f32[2,384,4]{1,2,0:T(4,128)} %param.51) | copy-start | bytes 36868
  687.0 52.2 %copy-start.138 = (f32[2,384,4]{1,2,0:T(4,128)S(1)}, f32[2,384,4]{1,2,0:T(4,128)}, u32[]{:S(2)}) copy-start(f32[2,384,4]{1,2,0:T(4,128)} %param.52) | copy-start | bytes 36868
  687.0 52.2 %copy-start.139 = (f32[2,384,4]{1,2,0:T(4,128)S(1)}, f32[2,384,4]{1,2,0:T(4,128)}, u32[]{:S(2)}) copy-start(f32[2,384,4]{1,2,0:T(4,128)} %param.53) | copy-start | bytes 36868
  687.0 315.3 %copy-start.34 = (f32[2,384,768]{2,1,0:T(8,128)S(1)}, f32[2,384,768]{2,1,0:T(8,128)}, u32[]{:S(2)}) copy-start(f32[2,384,768]{2,1,0:T(8,128)} %param.42) | copy-start | bytes 7077892
  687.0 322.1 %slice-start.6 = ((s8[9437184]{0:T(1024)(128)(4,1)}), s8[1048576]{0:T(1024)(128)(4,1)S(1)}, s32[]{:S(2)}) async-start(s8[9437184]{0:T(1024)(128)(4,1)} %bitcast.338), calls=%async_computation.26 | async-start | bytes 2097152
  (138 other events, 549.8 us)
Sparse Core Ops, SparseCore 0:
  12.8 15.3 all-gather.20
  30.3 10.3 all-gather.22
  42.9 15.6 all-gather.24
  60.5 15.6 all-gather.26
  78.1 13.8 all-gather.28
  94.0 10.3 all-gather.30
  106.6 15.5 all-gather.32
  124.3 15.5 all-gather.34
  463.7 11.6 reduce-scatter.9
  497.9 19.4 reduce-scatter.13
  542.5 19.8 reduce-scatter.11
  648.9 18.0 reduce-scatter.7
  669.8 8.7 reduce-scatter.15
  684.9 317.3 all-reduce.6
  1005.3 567.7 all-gather.36
